TPU v7x, 32 devices: a whole 2x2x4 slice. The times are simulated.
32 devices in a mesh: clip: 2 (over y), tm: 4 (over z), head: 2 (over x), sub: 2 (over core).
Axes of the slice: x: 2, y: 2, z: 4, core: 2. Of those that a mesh axis runs over, the one named last changes fastest.
Arguments:
- queries: bfloat16 [8, 256, 3072], P(('clip', 'tm'), None, ('head', 'sub')), parts along dimension 0, may hold values from -6 to 6, as said below
- keys: bfloat16 [8, 256, 3072], P(('clip', 'tm'), None, ('head', 'sub')), parts along dimension 0, may hold values from -6 to 6, as said below
- values: bfloat16 [8, 256, 3072], P(('clip', 'tm'), None, ('head', 'sub')), parts along dimension 0, may hold values from -6 to 6
- band_table: int32 [4, 4], replicated, may hold values from 0 to 3, as said below
- windows: int32 [7], replicated, may hold values from 1 to 128, as said below
- out_weight: bfloat16 [3072, 3072], P(('head', 'sub')), may hold values from -0.109375 to 0.109375
Outputs:
- mixed: bfloat16 [8, 256, 3072], P(('clip', 'tm'), ('head', 'sub')), parts along dimension 0
There are 2 independent parts, one for each index of `clip`. A program takes and returns all parts, laid end to end along the dimension named above; an argument that names none is the same for every part. Nothing has to cross between parts.
Inputs may be any that keep to these rules, and one draw needn't show every extreme that they name: `queries`: entries of normal law within the range; some rows may be aligned with some key rows. `keys`: entries of normal law within the range; some rows may be aligned with some query rows. `band_table`: Symmetric; 0 exactly on the diagonal; off the diagonal, for frames at distance d it is floor(log2 d) + 1 or one more, never above 6; the pair of frames 0 and 3 takes the one more (up to 6). windows[0] = 128; for k >= 1, windows[k] lies between max(1, 64 // 2**k) and max(that + 1, 128 // 2**k + 1) - 1.
All inputs are finite; a program needn't handle non-finite values.
Results may differ from a plain program's by a relative error of at most 0.015.
Values may be sent and summed in bfloat16 or wider, within the bound.
A program may use at most 64 MiB of HBM per device.

v0:
```python
import jax
import jax.numpy as jnp
from jax import lax
from jax.sharding import PartitionSpec as P

HEAD = 128


def local(queries, keys, values, band_table, windows, out_weight):
    frames, length, width = queries.shape
    heads = width // HEAD
    scale = HEAD ** (-0.5)
    here = lax.axis_index("tm") * frames
    query = queries[0].reshape(length, heads, HEAD)
    places = lax.iota(jnp.int32, length)
    gap = jnp.abs(places[:, None] - places[None, :])

    def absorb(carry, key_frame, value_frame, frame, usable):
        peak, total, numer = carry
        reach = windows[band_table[here, frame]]
        allowed = (gap <= reach)[None] & usable
        scores = (
            jnp.einsum(
                "phd,qhd->hpq",
                query,
                key_frame.reshape(length, heads, HEAD),
                preferred_element_type=jnp.float32,
            )
            * scale
        )
        masked = jnp.where(allowed, scores, jnp.float32(-1e30))
        top = jnp.maximum(peak, jnp.max(masked, axis=-1))
        weights = jnp.where(allowed, jnp.exp(scores - top[:, :, None]), jnp.float32(0.0))
        shrink = jnp.exp(peak - top)
        total = total * shrink + jnp.sum(weights, axis=-1)
        added = jnp.einsum(
            "hpq,qhd->phd",
            weights.astype(jnp.bfloat16),
            value_frame.reshape(length, heads, HEAD),
            preferred_element_type=jnp.float32,
        )
        numer = numer * jnp.transpose(shrink)[:, :, None] + added
        return (top, total, numer)

    carry = (
        jnp.full((heads, length), -1e30, jnp.float32),
        jnp.zeros((heads, length), jnp.float32),
        jnp.zeros((length, heads, HEAD), jnp.float32),
    )
    skipped = -1
    state = carry
    key_part = lax.all_gather(keys, "tm", axis=0, tiled=True)
    value_part = lax.all_gather(values, "tm", axis=0, tiled=True)

    def advance(inner, item):
        key_frame, value_frame, offset = item
        usable = jnp.abs(offset - here) > skipped
        return (absorb(inner, key_frame, value_frame, offset, usable), None)

    state, unused = lax.scan(
        advance, state, (key_part, value_part, lax.iota(jnp.int32, key_part.shape[0]))
    )
    carry = state
    peak, total, numer = carry
    attended = (
        (numer / jnp.transpose(total)[:, :, None]).astype(jnp.bfloat16).reshape(length, width)
    )
    mixed = lax.psum_scatter(
        jnp.dot(attended, out_weight, preferred_element_type=jnp.float32).astype(jnp.bfloat16),
        ("head", "sub"),
        scatter_dimension=0,
        tiled=True,
    )
    return mixed[None]


def solution(mesh):
    return jax.shard_map(
        local,
        mesh=mesh,
        in_specs=(
            P(("clip", "tm"), None, ("head", "sub")),
            P(("clip", "tm"), None, ("head", "sub")),
            P(("clip", "tm"), None, ("head", "sub")),
            P(),
            P(),
            P(("head", "sub"), None),
        ),
        out_specs=P(("clip", "tm"), ("head", "sub"), None),
        check_vma=False,
    )
```

profile of v0, /device:TPU:0, one launch (start us, length us, event | category | flops | bytes accessed | tf_op | source)
XLA Modules:
  0.0 169.9 jit_solution(7781933475861130219)
XLA Ops:
  6.5 0.0 copy-start
  6.5 0.0 all-gather.3.cloned.1.call-start
  6.5 0.7 all-gather.3.cloned.1.call-update
  7.3 0.0 all-gather.5.cloned.1.call-start
  7.3 0.7 all-gather.5.cloned.1.call-update
  8.0 0.0 reduce-scatter.2.cloned.1.call-start
  8.1 1.2 copy.17
  9.3 0.9 copy.19
  10.2 38.5 %all-gather.3.cloned.1.call-done = bf16[4,256,768]{2,1,0:T(8,128)(2,1)} async-done(((bf16[1,256,768]{2,1,0:T(8,128)(2,1)}), bf16[4,256,768]{2,1,0:T(8,128)(2,1)}) %all-gather.3.cloned.1.call-update) | async-done | bytes 1572880 | tf_op jit(solution)/shard_map/all_gather | solution.py:52
  48.7 37.5 %all-gather.5.cloned.1.call-done = bf16[4,256,768]{2,1,0:T(8,128)(2,1)} async-done(((bf16[1,256,768]{2,1,0:T(8,128)(2,1)}), bf16[4,256,768]{2,1,0:T(8,128)(2,1)}) %all-gather.5.cloned.1.call-update) | async-done | bytes 1572880 | tf_op jit(solution)/shard_map/all_gather | solution.py:53
  86.2 0.0 copy-done
  86.2 45.1 %while.17 = (s32[]{:T(128)}, f32[6,256]{1,0:T(8,128)S(1)}, f32[6,256]{1,0:T(8,128)S(1)}, f32[256,6,128]{0,2,1:T(8,128)S(1)}, s32[4]{0:T(128)S(1)}, /*index=5*/s3...) while((s32[]{:T(128)}, f32[6,256]{1,0:T(8,128)S(1)}, ...), condition=%wide.region_3.4_spmd.clone, body=%wide.region_0.3_spmd.clone.sunk | while | flops 205726720 | bytes 10977591 | solution.py:60
  86.2 0.6 dynamic_slice.39
  88.5 1.3 dynamic_slice.40
  91.7 0.6 dynamic_slice.41
  92.9 0.7 fusion.35
  93.6 1.2 constant_dynamic-slice_fusion.3
  94.8 0.2 copy.27
  94.9 1.5 fusion.36
  96.4 0.2 copy.28
  96.6 0.5 fusion.40
  97.1 0.3 fusion.38
  97.5 0.6 dynamic_slice.39
  99.7 1.3 dynamic_slice.40
  103.0 0.6 dynamic_slice.41
  104.2 0.7 fusion.35
  104.9 1.2 constant_dynamic-slice_fusion.3
  106.0 0.2 copy.27
  106.2 1.5 fusion.36
  107.7 0.2 copy.28
  107.9 0.5 fusion.40
  108.4 0.3 fusion.38
  108.7 0.6 dynamic_slice.39
  111.0 1.3 dynamic_slice.40
  114.2 0.6 dynamic_slice.41
  115.4 0.7 fusion.35
  116.2 1.2 constant_dynamic-slice_fusion.3
  117.3 0.2 copy.27
  117.5 1.5 fusion.36
  119.0 0.2 copy.28
  119.2 0.5 fusion.40
  119.7 0.3 fusion.38
  120.0 0.6 dynamic_slice.39
  122.3 1.3 dynamic_slice.40
  125.5 0.6 dynamic_slice.41
  126.7 0.7 fusion.35
  127.4 1.2 constant_dynamic-slice_fusion.3
  128.6 0.2 copy.27
  128.8 1.4 fusion.36
  130.3 0.2 copy.28
  130.4 0.5 fusion.40
  131.0 0.3 fusion.38
  131.3 0.1 divide_convert_fusion
  131.4 4.9 %convolution_convert_fusion = bf16[256,3072]{1,0:T(8,128)(2,1)} fusion(bf16[256,768]{0,1:T(8,128)(2,1)S(1)} %bitcast.62, bf16[768,3072]{1,0:T(8,128)(2,1)} %param.13), kind=kOutput, calls=%fused_computation.25 | convolution fusion | flops 1208745984 | bytes 6684672 | tf_op jit(solution)/shard_map/dot_general | solution.py:69
  136.3 0.0 reduce-scatter.2.cloned.1.call-update
  136.3 27.0 %reduce-scatter.2.cloned.1.call-done = bf16[64,3072]{1,0:T(8,128)(2,1)} async-done(((bf16[256,3072]{1,0:T(8,128)(2,1)}), bf16[64,3072]{1,0:T(8,128)(2,1)}) %reduce-scatter.2.cloned.1.call-update) | async-done | bytes 393232 | tf_op jit(solution)/shard_map/reduce_scatter | solution.py:68
  (16 shorter events, 0.1 us)
Async XLA Ops:
  6.5 79.6 %copy-start = (s32[7]{0:T(128)S(1)}, s32[7]{0:T(128)}, u32[]{:S(2)}) copy-start(s32[7]{0:T(128)} %param.12) | copy-start | bytes 88
  6.5 42.1 %all-gather.3.cloned.1.call-start = ((), (), s32[]{:S(2)}) async-start(), calls=%async_computation.1 | async-start | bytes 1966080 | tf_op jit(solution)/shard_map/all_gather | solution.py:52
  7.3 78.9 %all-gather.5.cloned.1.call-start = ((), (), s32[]{:S(2)}) async-start(), calls=%async_computation.2 | async-start | bytes 1966080 | tf_op jit(solution)/shard_map/all_gather | solution.py:53
  8.0 155.3 %reduce-scatter.2.cloned.1.call-start = ((), (), s32[]{:S(2)}) async-start(), calls=%async_computation.3 | async-start | bytes 1966080 | tf_op jit(solution)/shard_map/reduce_scatter | solution.py:68
Sparse Core Ops, SparseCore 0:
  8.9 39.7 all-gather.2
  50.2 35.8 all-gather.4
  136.4 26.8 reduce-scatter.1
where the time goes:
time: 171 us; the launch traced here: 170 us
  waiting for transfers between devices  104 us (61%)
  local copies, waits for them, and re-layouts  18.4 us (11%)
  loops' own time  16.9 us (10%)
  between operations  13.2 us (8%)
  matrix products  12.8 us (7%)
  other arithmetic  4.12 us (2%)
    all_gather x1, waiting for transfers between devices, local(): key_part = lax.all_gather(keys, 'tm', axis=0, tiled=True)  38.5 us
    all_gather x1, waiting for transfers between devices, local(): value_part = lax.all_gather(values, 'tm', axis=0, tiled=True)  37.5 us
    reduce_scatter x1, waiting for transfers between devices, local(): lax.psum_scatter(jnp.dot(attended, out_weight, preferred_element_type=jnp...  27 us
    another operation x1, loops' own time, local(): lax.scan(advance, state, (key_part, value_part, lax.iota(jnp.int32, key_p...  16.9 us
    dynamic_slice x16, local copies, waits for them, and re-layouts, local(): lax.scan(advance, state, (key_part, value_part, lax.iota(jnp.int32, key_p...  8.4 us
    dynamic_slice x8, local copies, waits for them, and re-layouts, absorb(): reach = windows[band_table[here, frame]]  7.86 us
    dot_general x4, matrix products, absorb(): jnp.einsum('phd,qhd->hpq', query, key_frame.reshape(length, heads, HEAD),...  5.81 us
    dot_general x1, matrix products, local(): jnp.dot(attended, out_weight, preferred_element_type=jnp.float32)  4.92 us
  transfers between devices with their start and end apart: 3, of which 3 were waited for; matrix products, arithmetic and copies ran while one was open for 1% of the time, Pallas kernels for 0%

commit v1 on v0

--- a/solution.py
+++ b/solution.py
@@ -1,9 +1,14 @@
+import functools
+
 import jax
 import jax.numpy as jnp
 from jax import lax
+from jax.experimental import pallas as pl
+from jax.experimental.pallas import tpu as pltpu
 from jax.sharding import PartitionSpec as P
 
 HEAD = 128
+MESH = pl.DeviceIdType.MESH
 
 
 def local(queries, keys, values, band_table, windows, out_weight):
@@ -74,9 +79,259 @@
     return mixed[None]
 
 
+def fused_kernel(
+    n, chunks, q_hbm, k_hbm, v_hbm, band, windows, w_hbm, out_ref,
+    buf, weight, done, att, send_a, recv_a, send_b, recv_b, acc,
+    in_send, in_recv, back_send, back_recv, a_send, a_recv, b_send, b_recv, w_sem,
+):
+    frame = lax.axis_index("tm")
+    row = lax.axis_index("head")
+    core = lax.axis_index("sub")
+    length = q_hbm.shape[1]
+    heads = 2 * n - 2
+    owner = [(h + 1) // 2 for h in range(heads)]
+    slot = [1 if h > 0 and h % 2 == 0 else 0 for h in range(heads)]
+    scale = HEAD ** (-0.5)
+
+    barrier = pltpu.get_barrier_semaphore()
+    for step in range(1, n):
+        pl.semaphore_signal(
+            barrier, inc=1, device_id={"tm": lax.rem(frame + step, n)}, device_id_type=MESH
+        )
+    pl.semaphore_signal(barrier, inc=1, device_id={"head": 1 - row}, device_id_type=MESH)
+    pl.semaphore_signal(barrier, inc=1, device_id={"sub": 1 - core}, device_id_type=MESH)
+    pl.semaphore_wait(barrier, n + 1)
+
+    sources = (q_hbm, k_hbm, v_hbm)
+    order = [h for h in range(heads) if slot[h] == 0] + [h for h in range(heads) if slot[h] == 1]
+
+    def outgoing(h, a):
+        return pltpu.make_async_remote_copy(
+            src_ref=sources[a].at[0, :, h * HEAD : (h + 1) * HEAD],
+            dst_ref=buf.at[slot[h], a, frame],
+            send_sem=in_send.at[h, a],
+            recv_sem=in_recv.at[slot[h], a, frame],
+            device_id={"tm": owner[h]},
+            device_id_type=MESH,
+        )
+
+    for h in order:
+
+        @pl.when(frame != owner[h])
+        def _():
+            for a in range(3):
+                outgoing(h, a).start()
+
+        @pl.when(frame == owner[h])
+        def _():
+            for a in range(3):
+                pltpu.make_async_copy(
+                    sources[a].at[0, :, h * HEAD : (h + 1) * HEAD],
+                    buf.at[slot[h], a, frame],
+                    in_recv.at[slot[h], a, frame],
+                ).start()
+
+    load_weight = pltpu.make_async_copy(w_hbm, weight, w_sem)
+    load_weight.start()
+
+    gap = jnp.abs(
+        lax.broadcasted_iota(jnp.int32, (length, length), 0)
+        - lax.broadcasted_iota(jnp.int32, (length, length), 1)
+    )
+
+    def returning(s, h, i):
+        return pltpu.make_async_remote_copy(
+            src_ref=done.at[s, i],
+            dst_ref=att.at[:, pl.ds(pl.multiple_of(h * HEAD, HEAD), HEAD)],
+            send_sem=back_send.at[s, i],
+            recv_sem=back_recv.at[h],
+            device_id={"tm": i},
+            device_id_type=MESH,
+        )
+
+    def attend(s, h):
+        for j in range(n):
+            for a in range(3):
+                pltpu.make_async_copy(buf.at[s, a, j], buf.at[s, a, j], in_recv.at[s, a, j]).wait()
+
+        def one(step, carry):
+            i = lax.rem(frame + 1 + step, n)
+            query = buf[s, 0, i]
+            parts = []
+            top = None
+            for j in range(n):
+                score = lax.dot_general(
+                    query, buf[s, 1, j], (((1,), (1,)), ((), ())),
+                    preferred_element_type=jnp.float32,
+                ) * scale
+                score = jnp.where(gap <= windows[band[i, j]], score, jnp.float32(-1e30))
+                peak = jnp.max(score, axis=-1, keepdims=True)
+                top = peak if top is None else jnp.maximum(top, peak)
+                parts.append(score)
+            total = None
+            numer = None
+            for j in range(n):
+                part = jnp.exp(parts[j] - top)
+                added = jnp.sum(part, axis=-1, keepdims=True)
+                product = jnp.dot(
+                    part.astype(jnp.bfloat16), buf[s, 2, j], preferred_element_type=jnp.float32
+                )
+                total = added if total is None else total + added
+                numer = product if numer is None else numer + product
+            result = (numer / total).astype(jnp.bfloat16)
+
+            @pl.when(i != frame)
+            def _():
+                done[s, i] = result
+                returning(s, h, i).start()
+
+            @pl.when(i == frame)
+            def _():
+                att[:, pl.ds(pl.multiple_of(h * HEAD, HEAD), HEAD)] = result
+
+            return carry
+
+        lax.fori_loop(0, n, one, 0)
+
+    first = 2 * frame - (frame + n - 1) // n
+    second = 2 * frame
+    both = jnp.logical_and(frame > 0, frame < n - 1)
+    attend(0, first)
+
+    @pl.when(both)
+    def _():
+        attend(1, second)
+
+    load_weight.wait()
+    for h in range(heads):
+
+        @pl.when(frame != owner[h])
+        def _():
+            here = att.at[:, h * HEAD : (h + 1) * HEAD]
+            pltpu.make_async_copy(here, here, back_recv.at[h]).wait()
+
+    block = length // 4
+    width = weight.shape[1] // chunks
+
+    def rows(who):
+        return jnp.concatenate(
+            [
+                att[pl.ds(pl.multiple_of(r * 2 * block + who * block, block), block), :]
+                for r in (row, 1 - row)
+            ],
+            axis=0,
+        )
+
+    def give_a(c):
+        return pltpu.make_async_remote_copy(
+            src_ref=send_a.at[c], dst_ref=recv_a.at[c],
+            send_sem=a_send.at[c], recv_sem=a_recv.at[c],
+            device_id={"sub": 1 - core}, device_id_type=MESH,
+        )
+
+    def give_b(c):
+        return pltpu.make_async_remote_copy(
+            src_ref=send_b.at[c], dst_ref=recv_b.at[c],
+            send_sem=b_send.at[c], recv_sem=b_recv.at[c],
+            device_id={"head": 1 - row}, device_id_type=MESH,
+        )
+
+    theirs = rows(1 - core)
+    for c in range(chunks):
+        send_a[c] = jnp.dot(
+            theirs, weight[:, c * width : (c + 1) * width], preferred_element_type=jnp.float32
+        ).astype(jnp.bfloat16)
+        give_a(c).start()
+    mine = rows(core)
+    for c in range(chunks):
+        own = jnp.dot(
+            mine, weight[:, c * width : (c + 1) * width], preferred_element_type=jnp.float32
+        )
+        give_a(c).wait_recv()
+        own = own + recv_a[c].astype(jnp.float32)
+        send_b[c] = own[block:].astype(jnp.bfloat16)
+        give_b(c).start()
+        acc[c] = own[:block]
+    for c in range(chunks):
+        give_b(c).wait_recv()
+        out_ref[:, c * width : (c + 1) * width] = (
+            acc[c] + recv_b[c].astype(jnp.float32)
+        ).astype(jnp.bfloat16)
+
+    for c in range(chunks):
+        give_a(c).wait_send()
+        give_b(c).wait_send()
+    for h in range(heads):
+
+        @pl.when(frame != owner[h])
+        def _():
+            for a in range(3):
+                outgoing(h, a).wait_send()
+
+    for i in range(n):
+
+        @pl.when(i != frame)
+        def _():
+            returning(0, first, i).wait_send()
+
+        @pl.when(jnp.logical_and(both, i != frame))
+        def _():
+            returning(1, second, i).wait_send()
+
+
+def fused(n, queries, keys, values, band_table, windows, out_weight):
+    length, width = queries.shape[1:]
+    columns = out_weight.shape[1]
+    heads = width // HEAD
+    block = length // 4
+    chunks = 4
+    part = columns // chunks
+    anywhere = pl.BlockSpec(memory_space=pl.ANY)
+    scalar = pl.BlockSpec(memory_space=pltpu.SMEM)
+    dma = pltpu.SemaphoreType.DMA
+    mixed = pl.pallas_call(
+        functools.partial(fused_kernel, n, chunks),
+        out_shape=jax.ShapeDtypeStruct((block, columns), jnp.bfloat16),
+        in_specs=[anywhere, anywhere, anywhere, scalar, scalar, anywhere],
+        out_specs=pl.BlockSpec(memory_space=pltpu.VMEM),
+        scratch_shapes=[
+            pltpu.VMEM((2, 3, n, length, HEAD), jnp.bfloat16),
+            pltpu.VMEM(out_weight.shape, jnp.bfloat16),
+            pltpu.VMEM((2, n, length, HEAD), jnp.bfloat16),
+            pltpu.VMEM((length, width), jnp.bfloat16),
+            pltpu.VMEM((chunks, 2 * block, part), jnp.bfloat16),
+            pltpu.VMEM((chunks, 2 * block, part), jnp.bfloat16),
+            pltpu.VMEM((chunks, block, part), jnp.bfloat16),
+            pltpu.VMEM((chunks, block, part), jnp.bfloat16),
+            pltpu.VMEM((chunks, block, part), jnp.float32),
+            dma((heads, 3)),
+            dma((2, 3, n)),
+            dma((2, n)),
+            dma((heads,)),
+            dma((chunks,)),
+            dma((chunks,)),
+            dma((chunks,)),
+            dma((chunks,)),
+            dma,
+        ],
+        compiler_params=pltpu.CompilerParams(
+            collective_id=0, has_side_effects=True, vmem_limit_bytes=40 * 1024 * 1024
+        ),
+    )(queries, keys, values, band_table, windows, out_weight)
+    return mixed[None]
+
+
 def solution(mesh):
+    n = mesh.shape["tm"]
+
+    def step(queries, keys, values, band_table, windows, out_weight):
+        paired = mesh.shape["head"] == 2 and mesh.shape["sub"] == 2
+        if n > 2 and paired and queries.shape[0] == 1 and queries.shape[2] == (2 * n - 2) * HEAD:
+            return fused(n, queries, keys, values, band_table, windows, out_weight)
+        return local(queries, keys, values, band_table, windows, out_weight)
+
     return jax.shard_map(
-        local,
+        step,
         mesh=mesh,
         in_specs=(
             P(("clip", "tm"), None, ("head", "sub")),

time: 171 us -> 62.3 us (0.36)
  waiting for transfers between devices: 104 us -> 0 us
  Pallas kernels: 0 us -> 54.6 us
  loops' own time: 16.9 us -> 0 us
  between operations: 13.2 us -> 0.02 us
  matrix products: 12.8 us -> 0 us
  local copies, waits for them, and re-layouts: 18.4 us -> 7.41 us
  other arithmetic: 4.12 us -> 0 us
    all_gather x2 -> x0, waiting for transfers between devices: 76 us -> none  [the longest x1 38.5 us: local(): key_part = lax.all_gather(keys, 'tm', axis=0, tiled=True)]
    pallas_call x0 -> x1, Pallas kernels: none -> 54.6 us  [fused(): pl.pallas_call(functools.partial(fused_kernel, n, chunks), out_shape=jax....]
    reduce_scatter x1 -> x0, waiting for transfers between devices: 27 us -> none  [local(): lax.psum_scatter(jnp.dot(attended, out_weight, preferred_element_type=jnp...]
    another operation x1 -> x0, loops' own time: 16.9 us -> none  [local(): lax.scan(advance, state, (key_part, value_part, lax.iota(jnp.int32, key_p...]
    dynamic_slice x24 -> x0, local copies, waits for them, and re-layouts: 16.3 us -> none  [the longest x16 8.4 us: local(): lax.scan(advance, state, (key_part, value_part, lax.iota(jnp.int32, key_p...]
    dot_general x9 -> x0, matrix products: 12.8 us -> none  [the longest x4 5.81 us: absorb(): jnp.einsum('phd,qhd->hpq', query, key_frame.reshape(length, heads, HEAD),...]
    unnamed x4 -> x13, local copies, waits for them, and re-layouts: 2.09 us -> 7.41 us
    and x4 -> x0, other arithmetic: 2.81 us -> none  [absorb(): allowed = (gap <= reach)[None] & usable]
  transfers between devices with their start and end apart: 3 -> 0, of which waited for: 3 -> 0; matrix products, arithmetic and copies ran while one was open for 1% -> 0% of each run, Pallas kernels for 0% -> 0%
where the time goes in v1:
time: 62.3 us; the launch traced here: 62 us
  Pallas kernels  54.6 us (88%)
  local copies, waits for them, and re-layouts  7.41 us (12%)
    pallas_call x1, Pallas kernels, fused(): pl.pallas_call(functools.partial(fused_kernel, n, chunks), out_shape=jax....  54.6 us
    unnamed x13, local copies, waits for them, and re-layouts  7.41 us

profile of v1, /device:TPU:0, one launch (start us, length us, event | category | flops | bytes accessed | tf_op | source)
XLA Modules:
  0.0 62.0 jit_solution(13472235348301076873)
XLA Ops:
  0.0 0.0 copy-start
  0.0 2.3 %copy-done = bf16[768,3072]{1,0:T(8,128)(2,1)S(1)} copy-done((bf16[768,3072]{1,0:T(8,128)(2,1)S(1)}, bf16[768,3072]{1,0:T(8,128)(2,1)}, u32[]{:S(2)}) %copy-start) | copy-done | bytes 4718616
  2.3 0.0 copy-start.1
  2.3 1.0 %copy-done.1 = bf16[1,256,768]{2,1,0:T(8,128)(2,1)S(1)} copy-done((bf16[1,256,768]{2,1,0:T(8,128)(2,1)S(1)}, bf16[1,256,768]{2,1,0:T(8,128)(2,1)}, u32[]{:S(2)}) %copy-start.1) | copy-done | bytes 393240
  3.3 0.0 copy-start.2
  3.3 1.0 %copy-done.2 = bf16[1,256,768]{2,1,0:T(8,128)(2,1)S(1)} copy-done((bf16[1,256,768]{2,1,0:T(8,128)(2,1)S(1)}, bf16[1,256,768]{2,1,0:T(8,128)(2,1)}, u32[]{:S(2)}) %copy-start.2) | copy-done | bytes 393240
  4.3 0.0 copy-start.3
  4.3 1.0 %copy-done.3 = bf16[1,256,768]{2,1,0:T(8,128)(2,1)S(1)} copy-done((bf16[1,256,768]{2,1,0:T(8,128)(2,1)S(1)}, bf16[1,256,768]{2,1,0:T(8,128)(2,1)}, u32[]{:S(2)}) %copy-start.3) | copy-done | bytes 393240
  5.3 0.0 copy-start.4
  5.3 0.7 %copy-done.4 = s32[4,4]{1,0:T(4,128)S(1)} copy-done((s32[4,4]{1,0:T(4,128)S(1)}, s32[4,4]{1,0:T(4,128)}, u32[]{:S(2)}) %copy-start.4) | copy-done | bytes 88
  6.0 0.0 copy-start.5
  6.0 0.7 %copy-done.5 = s32[7]{0:T(128)S(1)} copy-done((s32[7]{0:T(128)S(1)}, s32[7]{0:T(128)}, u32[]{:S(2)}) %copy-start.5) | copy-done | bytes 52
  6.7 54.6 %shard_map.64 = bf16[64,3072]{1,0:T(8,128)(2,1)S(1)} custom-call(bf16[1,256,768]{2,1,0:T(8,128)(2,1)S(1)} %copy-done.1, bf16[1,256,768]{2,1,0:T(8,128)(2,1)S(1)} %copy-done.2, bf16[1,256,768]{2,1,0:T(8,128)(2,1)S(1)} %copy-done.3, s32[4,4]{1,0:T(4,128)S(1)} %copy-done.4, s32[7]{0:T(128)S(1)} %copy-done.5, bf16[768,3072]{1,0:T(8,128)(2,1)S(1)} %copy-done), custom_call_target="tpu_custom_call" | custom-call | tf_op jit(solution)/shard_map/pallas_call | solution.py:292
  61.3 0.7 %copy.8 = bf16[1,64,3072]{2,1,0:T(8,128)(2,1)} copy(bf16[1,64,3072]{2,1,0:T(8,128)(2,1)S(1)} %bitcast.1) | data formatting | bytes 786432
Async XLA Ops:
  0.0 2.3 %copy-start = (bf16[768,3072]{1,0:T(8,128)(2,1)S(1)}, bf16[768,3072]{1,0:T(8,128)(2,1)}, u32[]{:S(2)}) copy-start(bf16[768,3072]{1,0:T(8,128)(2,1)} %w_hbm.1) | copy-start | bytes 14155780
  2.3 1.0 %copy-start.1 = (bf16[1,256,768]{2,1,0:T(8,128)(2,1)S(1)}, bf16[1,256,768]{2,1,0:T(8,128)(2,1)}, u32[]{:S(2)}) copy-start(bf16[1,256,768]{2,1,0:T(8,128)(2,1)} %q_hbm.1) | copy-start | bytes 1179652
  3.3 1.0 %copy-start.2 = (bf16[1,256,768]{2,1,0:T(8,128)(2,1)S(1)}, bf16[1,256,768]{2,1,0:T(8,128)(2,1)}, u32[]{:S(2)}) copy-start(bf16[1,256,768]{2,1,0:T(8,128)(2,1)} %k_hbm.1) | copy-start | bytes 1179652
  4.3 1.0 %copy-start.3 = (bf16[1,256,768]{2,1,0:T(8,128)(2,1)S(1)}, bf16[1,256,768]{2,1,0:T(8,128)(2,1)}, u32[]{:S(2)}) copy-start(bf16[1,256,768]{2,1,0:T(8,128)(2,1)} %v_hbm.1) | copy-start | bytes 1179652
  5.3 0.7 %copy-start.4 = (s32[4,4]{1,0:T(4,128)S(1)}, s32[4,4]{1,0:T(4,128)}, u32[]{:S(2)}) copy-start(s32[4,4]{1,0:T(4,128)} %band.1) | copy-start | bytes 196
  6.0 0.7 %copy-start.5 = (s32[7]{0:T(128)S(1)}, s32[7]{0:T(128)}, u32[]{:S(2)}) copy-start(s32[7]{0:T(128)} %windows.1) | copy-start | bytes 88

commit v2 on v1

--- a/solution.py
+++ b/solution.py
@@ -80,9 +80,9 @@
 
 
 def fused_kernel(
-    n, chunks, q_hbm, k_hbm, v_hbm, band, windows, w_hbm, out_ref,
-    buf, weight, done, att, send_a, recv_a, send_b, recv_b, acc,
-    in_send, in_recv, back_send, back_recv, a_send, a_recv, b_send, b_recv, w_sem,
+    n, pieces, chunks, q_hbm, k_hbm, v_hbm, band_hbm, windows_hbm, w_hbm, out_ref,
+    band, windows, buf, weight, done, att, send_a, recv_a, send_b, recv_b, acc, own,
+    in_send, in_recv, back_send, back_recv, a_send, a_recv, b_send, b_recv, w_sem, table_sem,
 ):
     frame = lax.axis_index("tm")
     row = lax.axis_index("head")
@@ -103,7 +103,7 @@
     pl.semaphore_wait(barrier, n + 1)
 
     sources = (q_hbm, k_hbm, v_hbm)
-    order = [h for h in range(heads) if slot[h] == 0] + [h for h in range(heads) if slot[h] == 1]
+    low = frame < n // 2
 
     def outgoing(h, a):
         return pltpu.make_async_remote_copy(
@@ -115,12 +115,22 @@
             device_id_type=MESH,
         )
 
-    for h in order:
-
-        @pl.when(frame != owner[h])
+    def send_head(h, ready):
+        @pl.when(jnp.logical_and(ready, frame != owner[h]))
         def _():
             for a in range(3):
                 outgoing(h, a).start()
+
+    for s in range(2):
+        below = [h for h in range(heads) if slot[h] == s and owner[h] < n // 2]
+        above = [h for h in reversed(range(heads)) if slot[h] == s and owner[h] >= n // 2]
+        for h in above:
+            send_head(h, low)
+        for h in below:
+            send_head(h, frame >= 0)
+        for h in above:
+            send_head(h, jnp.logical_not(low))
+    for h in range(heads):
 
         @pl.when(frame == owner[h])
         def _():
@@ -133,30 +143,46 @@
 
     load_weight = pltpu.make_async_copy(w_hbm, weight, w_sem)
     load_weight.start()
-
-    gap = jnp.abs(
-        lax.broadcasted_iota(jnp.int32, (length, length), 0)
-        - lax.broadcasted_iota(jnp.int32, (length, length), 1)
-    )
-
-    def returning(s, h, i):
+    tables = (
+        pltpu.make_async_copy(band_hbm, band, table_sem.at[0]),
+        pltpu.make_async_copy(windows_hbm, windows, table_sem.at[1]),
+    )
+    for table in tables:
+        table.start()
+
+    for table in tables:
+        table.wait()
+    block = length // 4
+    slab = block // pieces
+    height = 4 * slab
+    spot = lax.broadcasted_iota(jnp.int32, (height, length), 0)
+    spot = (spot // slab) * block + lax.rem(spot, slab)
+    spot = spot - lax.broadcasted_iota(jnp.int32, (height, length), 1)
+
+    def returning(s, h, p, i):
         return pltpu.make_async_remote_copy(
-            src_ref=done.at[s, i],
-            dst_ref=att.at[:, pl.ds(pl.multiple_of(h * HEAD, HEAD), HEAD)],
-            send_sem=back_send.at[s, i],
-            recv_sem=back_recv.at[h],
+            src_ref=done.at[s, p, i],
+            dst_ref=att.at[p, :, pl.ds(pl.multiple_of(h * HEAD, HEAD), HEAD)],
+            send_sem=back_send.at[s, p, i],
+            recv_sem=back_recv.at[p, h],
             device_id={"tm": i},
             device_id_type=MESH,
         )
 
-    def attend(s, h):
+    def arrive(s):
         for j in range(n):
             for a in range(3):
                 pltpu.make_async_copy(buf.at[s, a, j], buf.at[s, a, j], in_recv.at[s, a, j]).wait()
 
+    def attend(s, h, p):
+        gap = jnp.abs(spot + p * slab)
+
         def one(step, carry):
             i = lax.rem(frame + 1 + step, n)
-            query = buf[s, 0, i]
+            query = jnp.concatenate(
+                [buf[s, 0, i, b * block + p * slab : b * block + (p + 1) * slab, :] for b in range(4)],
+                axis=0,
+            )
             parts = []
             top = None
             for j in range(n):
@@ -182,12 +208,12 @@
 
             @pl.when(i != frame)
             def _():
-                done[s, i] = result
-                returning(s, h, i).start()
+                done[s, p, i] = result
+                returning(s, h, p, i).start()
 
             @pl.when(i == frame)
             def _():
-                att[:, pl.ds(pl.multiple_of(h * HEAD, HEAD), HEAD)] = result
+                att[p, :, pl.ds(pl.multiple_of(h * HEAD, HEAD), HEAD)] = result
 
             return carry
 
@@ -196,71 +222,81 @@
     first = 2 * frame - (frame + n - 1) // n
     second = 2 * frame
     both = jnp.logical_and(frame > 0, frame < n - 1)
-    attend(0, first)
+    arrive(0)
+    attend(0, first, 0)
 
     @pl.when(both)
     def _():
-        attend(1, second)
+        arrive(1)
+        attend(1, second, 0)
+
+    for p in range(1, pieces):
+        attend(0, first, p)
+
+        @pl.when(both)
+        def _():
+            attend(1, second, p)
 
     load_weight.wait()
-    for h in range(heads):
-
-        @pl.when(frame != owner[h])
-        def _():
-            here = att.at[:, h * HEAD : (h + 1) * HEAD]
-            pltpu.make_async_copy(here, here, back_recv.at[h]).wait()
-
-    block = length // 4
     width = weight.shape[1] // chunks
 
-    def rows(who):
+    def rows(p, who):
         return jnp.concatenate(
             [
-                att[pl.ds(pl.multiple_of(r * 2 * block + who * block, block), block), :]
+                att[p, pl.ds(pl.multiple_of((r * 2 + who) * slab, slab), slab), :]
                 for r in (row, 1 - row)
             ],
             axis=0,
         )
 
-    def give_a(c):
+    def give_a(p, c):
         return pltpu.make_async_remote_copy(
-            src_ref=send_a.at[c], dst_ref=recv_a.at[c],
-            send_sem=a_send.at[c], recv_sem=a_recv.at[c],
+            src_ref=send_a.at[p, c], dst_ref=recv_a.at[p, c],
+            send_sem=a_send.at[p, c], recv_sem=a_recv.at[p, c],
             device_id={"sub": 1 - core}, device_id_type=MESH,
         )
 
-    def give_b(c):
+    def give_b(p, c):
         return pltpu.make_async_remote_copy(
-            src_ref=send_b.at[c], dst_ref=recv_b.at[c],
-            send_sem=b_send.at[c], recv_sem=b_recv.at[c],
+            src_ref=send_b.at[p, c], dst_ref=recv_b.at[p, c],
+            send_sem=b_send.at[p, c], recv_sem=b_recv.at[p, c],
             device_id={"head": 1 - row}, device_id_type=MESH,
         )
 
-    theirs = rows(1 - core)
-    for c in range(chunks):
-        send_a[c] = jnp.dot(
-            theirs, weight[:, c * width : (c + 1) * width], preferred_element_type=jnp.float32
-        ).astype(jnp.bfloat16)
-        give_a(c).start()
-    mine = rows(core)
-    for c in range(chunks):
-        own = jnp.dot(
-            mine, weight[:, c * width : (c + 1) * width], preferred_element_type=jnp.float32
-        )
-        give_a(c).wait_recv()
-        own = own + recv_a[c].astype(jnp.float32)
-        send_b[c] = own[block:].astype(jnp.bfloat16)
-        give_b(c).start()
-        acc[c] = own[:block]
-    for c in range(chunks):
-        give_b(c).wait_recv()
-        out_ref[:, c * width : (c + 1) * width] = (
-            acc[c] + recv_b[c].astype(jnp.float32)
-        ).astype(jnp.bfloat16)
-
-    for c in range(chunks):
-        give_a(c).wait_send()
-        give_b(c).wait_send()
+    for p in range(pieces):
+        for h in range(heads):
+
+            @pl.when(frame != owner[h])
+            def _():
+                here = att.at[p, :, h * HEAD : (h + 1) * HEAD]
+                pltpu.make_async_copy(here, here, back_recv.at[p, h]).wait()
+
+        tokens = jnp.concatenate([rows(p, 1 - core), rows(p, core)], axis=0)
+        for c in range(chunks):
+            share = jnp.dot(
+                tokens, weight[:, c * width : (c + 1) * width], preferred_element_type=jnp.float32
+            )
+            send_a[p, c] = share[: 2 * slab].astype(jnp.bfloat16)
+            give_a(p, c).start()
+            own[c] = share[2 * slab :]
+        for c in range(chunks):
+            give_a(p, c).wait_recv()
+            both_cores = own[c] + recv_a[p, c].astype(jnp.float32)
+            send_b[p, c] = both_cores[slab:].astype(jnp.bfloat16)
+            give_b(p, c).start()
+            acc[p, c] = both_cores[:slab]
+
+    for p in range(pieces):
+        for c in range(chunks):
+            give_b(p, c).wait_recv()
+            out_ref[p * slab : (p + 1) * slab, c * width : (c + 1) * width] = (
+                acc[p, c] + recv_b[p, c].astype(jnp.float32)
+            ).astype(jnp.bfloat16)
+
+    for p in range(pieces):
+        for c in range(chunks):
+            give_a(p, c).wait_send()
+            give_b(p, c).wait_send()
     for h in range(heads):
 
         @pl.when(frame != owner[h])
@@ -272,11 +308,13 @@
 
         @pl.when(i != frame)
         def _():
-            returning(0, first, i).wait_send()
+            for p in range(pieces):
+                returning(0, first, p, i).wait_send()
 
         @pl.when(jnp.logical_and(both, i != frame))
         def _():
-            returning(1, second, i).wait_send()
+            for p in range(pieces):
+                returning(1, second, p, i).wait_send()
 
 
 def fused(n, queries, keys, values, band_table, windows, out_weight):
@@ -285,37 +323,42 @@
     heads = width // HEAD
     block = length // 4
     chunks = 4
+    pieces = 2
+    slab = block // pieces
     part = columns // chunks
     anywhere = pl.BlockSpec(memory_space=pl.ANY)
-    scalar = pl.BlockSpec(memory_space=pltpu.SMEM)
     dma = pltpu.SemaphoreType.DMA
     mixed = pl.pallas_call(
-        functools.partial(fused_kernel, n, chunks),
+        functools.partial(fused_kernel, n, pieces, chunks),
         out_shape=jax.ShapeDtypeStruct((block, columns), jnp.bfloat16),
-        in_specs=[anywhere, anywhere, anywhere, scalar, scalar, anywhere],
+        in_specs=[anywhere] * 6,
         out_specs=pl.BlockSpec(memory_space=pltpu.VMEM),
         scratch_shapes=[
+            pltpu.SMEM(band_table.shape, jnp.int32),
+            pltpu.SMEM(windows.shape, jnp.int32),
             pltpu.VMEM((2, 3, n, length, HEAD), jnp.bfloat16),
             pltpu.VMEM(out_weight.shape, jnp.bfloat16),
-            pltpu.VMEM((2, n, length, HEAD), jnp.bfloat16),
-            pltpu.VMEM((length, width), jnp.bfloat16),
-            pltpu.VMEM((chunks, 2 * block, part), jnp.bfloat16),
-            pltpu.VMEM((chunks, 2 * block, part), jnp.bfloat16),
-            pltpu.VMEM((chunks, block, part), jnp.bfloat16),
-            pltpu.VMEM((chunks, block, part), jnp.bfloat16),
-            pltpu.VMEM((chunks, block, part), jnp.float32),
+            pltpu.VMEM((2, pieces, n, 4 * slab, HEAD), jnp.bfloat16),
+            pltpu.VMEM((pieces, 4 * slab, width), jnp.bfloat16),
+            pltpu.VMEM((pieces, chunks, 2 * slab, part), jnp.bfloat16),
+            pltpu.VMEM((pieces, chunks, 2 * slab, part), jnp.bfloat16),
+            pltpu.VMEM((pieces, chunks, slab, part), jnp.bfloat16),
+            pltpu.VMEM((pieces, chunks, slab, part), jnp.bfloat16),
+            pltpu.VMEM((pieces, chunks, slab, part), jnp.float32),
+            pltpu.VMEM((chunks, 2 * slab, part), jnp.float32),
             dma((heads, 3)),
             dma((2, 3, n)),
-            dma((2, n)),
-            dma((heads,)),
-            dma((chunks,)),
-            dma((chunks,)),
-            dma((chunks,)),
-            dma((chunks,)),
+            dma((2, pieces, n)),
+            dma((pieces, heads)),
+            dma((pieces, chunks)),
+            dma((pieces, chunks)),
+            dma((pieces, chunks)),
+            dma((pieces, chunks)),
             dma,
+            dma((2,)),
         ],
         compiler_params=pltpu.CompilerParams(
-            collective_id=0, has_side_effects=True, vmem_limit_bytes=40 * 1024 * 1024
+            collective_id=0, has_side_effects=True, vmem_limit_bytes=60 * 1024 * 1024
         ),
     )(queries, keys, values, band_table, windows, out_weight)
     return mixed[None]

time: 62.3 us -> 55.9 us (0.90)
  local copies, waits for them, and re-layouts: 7.41 us -> 1.77 us
    unnamed x13 -> x1, local copies, waits for them, and re-layouts: 7.41 us -> 1.77 us
where the time goes in v2:
time: 55.9 us; the launch traced here: 55.8 us
  Pallas kernels  54 us (97%)
  local copies, waits for them, and re-layouts  1.77 us (3%)
    pallas_call x1, Pallas kernels, fused(): pl.pallas_call(functools.partial(fused_kernel, n, pieces, chunks), out_sh...  54 us
    unnamed x1, local copies, waits for them, and re-layouts  1.77 us

profile of v2, /device:TPU:0, one launch (start us, length us, event | category | flops | bytes accessed | tf_op | source)
XLA Modules:
  0.0 55.8 jit_solution(11187921100034689329)
XLA Ops:
  0.0 54.0 %shard_map.64 = bf16[64,3072]{1,0:T(8,128)(2,1)} custom-call(bf16[1,256,768]{2,1,0:T(8,128)(2,1)} %q_hbm.1, bf16[1,256,768]{2,1,0:T(8,128)(2,1)} %k_hbm.1, bf16[1,256,768]{2,1,0:T(8,128)(2,1)} %v_hbm.1, s32[4,4]{1,0:T(4,128)} %band_hbm.1, s32[7]{0:T(128)} %windows_hbm.1, bf16[768,3072]{1,0:T(8,128)(2,1)} %w_hbm.1), custom_call_target="tpu_custom_call" | custom-call | tf_op jit(solution)/shard_map/pallas_call | solution.py:331
  54.0 1.8 %copy.8 = bf16[1,64,3072]{2,1,0:T(8,128)(2,1)} copy(bf16[1,64,3072]{2,1,0:T(8,128)(2,1)} %bitcast.1) | data formatting | bytes 786432

commit v3 on v2

--- a/solution.py
+++ b/solution.py
@@ -81,13 +81,15 @@
 
 def fused_kernel(
     n, pieces, chunks, q_hbm, k_hbm, v_hbm, band_hbm, windows_hbm, w_hbm, out_ref,
-    band, windows, buf, weight, done, att, send_a, recv_a, send_b, recv_b, acc, own,
+    band, windows, asked, buf, weight, done, att, send_a, recv_a, send_b, recv_b, acc, own,
     in_send, in_recv, back_send, back_recv, a_send, a_recv, b_send, b_recv, w_sem, table_sem,
 ):
     frame = lax.axis_index("tm")
     row = lax.axis_index("head")
     core = lax.axis_index("sub")
-    length = q_hbm.shape[1]
+    length = k_hbm.shape[1]
+    block = length // 4
+    slab = block // pieces
     heads = 2 * n - 2
     owner = [(h + 1) // 2 for h in range(heads)]
     slot = [1 if h > 0 and h % 2 == 0 else 0 for h in range(heads)]
@@ -102,44 +104,57 @@
     pl.semaphore_signal(barrier, inc=1, device_id={"sub": 1 - core}, device_id_type=MESH)
     pl.semaphore_wait(barrier, n + 1)
 
-    sources = (q_hbm, k_hbm, v_hbm)
     low = frame < n // 2
 
+    def ends(h, a):
+        columns = slice(h * HEAD, (h + 1) * HEAD)
+        if a < 2:
+            return (k_hbm, v_hbm)[a].at[0, :, columns], buf.at[slot[h], a, frame]
+        p = a - 2
+        source = q_hbm.at[:, p * slab : (p + 1) * slab, columns]
+        return source, asked.at[slot[h], p, frame]
+
     def outgoing(h, a):
+        source, target = ends(h, a)
         return pltpu.make_async_remote_copy(
-            src_ref=sources[a].at[0, :, h * HEAD : (h + 1) * HEAD],
-            dst_ref=buf.at[slot[h], a, frame],
+            src_ref=source,
+            dst_ref=target,
             send_sem=in_send.at[h, a],
             recv_sem=in_recv.at[slot[h], a, frame],
             device_id={"tm": owner[h]},
             device_id_type=MESH,
         )
 
-    def send_head(h, ready):
+    def send_head(h, ready, which):
         @pl.when(jnp.logical_and(ready, frame != owner[h]))
         def _():
-            for a in range(3):
+            for a in which:
                 outgoing(h, a).start()
 
-    for s in range(2):
+    def send_slot(s, which):
         below = [h for h in range(heads) if slot[h] == s and owner[h] < n // 2]
         above = [h for h in reversed(range(heads)) if slot[h] == s and owner[h] >= n // 2]
         for h in above:
-            send_head(h, low)
+            send_head(h, low, which)
         for h in below:
-            send_head(h, frame >= 0)
+            send_head(h, frame >= 0, which)
         for h in above:
-            send_head(h, jnp.logical_not(low))
+            send_head(h, jnp.logical_not(low), which)
+
+    send_slot(0, (0, 1))
+    send_slot(1, (0, 1))
+    send_slot(0, (2,))
+    send_slot(1, (2,))
+    for p in range(1, pieces):
+        send_slot(0, (2 + p,))
+        send_slot(1, (2 + p,))
     for h in range(heads):
 
         @pl.when(frame == owner[h])
         def _():
-            for a in range(3):
-                pltpu.make_async_copy(
-                    sources[a].at[0, :, h * HEAD : (h + 1) * HEAD],
-                    buf.at[slot[h], a, frame],
-                    in_recv.at[slot[h], a, frame],
-                ).start()
+            for a in range(2 + pieces):
+                source, target = ends(h, a)
+                pltpu.make_async_copy(source, target, in_recv.at[slot[h], a, frame]).start()
 
     load_weight = pltpu.make_async_copy(w_hbm, weight, w_sem)
     load_weight.start()
@@ -152,8 +167,6 @@
 
     for table in tables:
         table.wait()
-    block = length // 4
-    slab = block // pieces
     height = 4 * slab
     spot = lax.broadcasted_iota(jnp.int32, (height, length), 0)
     spot = (spot // slab) * block + lax.rem(spot, slab)
@@ -169,25 +182,24 @@
             device_id_type=MESH,
         )
 
-    def arrive(s):
+    def arrive(s, p):
         for j in range(n):
-            for a in range(3):
+            for a in (0, 1) if p == 0 else ():
                 pltpu.make_async_copy(buf.at[s, a, j], buf.at[s, a, j], in_recv.at[s, a, j]).wait()
+            here = asked.at[s, p, j]
+            pltpu.make_async_copy(here, here, in_recv.at[s, 2 + p, j]).wait()
 
     def attend(s, h, p):
         gap = jnp.abs(spot + p * slab)
 
         def one(step, carry):
             i = lax.rem(frame + 1 + step, n)
-            query = jnp.concatenate(
-                [buf[s, 0, i, b * block + p * slab : b * block + (p + 1) * slab, :] for b in range(4)],
-                axis=0,
-            )
+            query = asked[s, p, i].reshape(height, HEAD)
             parts = []
             top = None
             for j in range(n):
                 score = lax.dot_general(
-                    query, buf[s, 1, j], (((1,), (1,)), ((), ())),
+                    query, buf[s, 0, j], (((1,), (1,)), ((), ())),
                     preferred_element_type=jnp.float32,
                 ) * scale
                 score = jnp.where(gap <= windows[band[i, j]], score, jnp.float32(-1e30))
@@ -200,7 +212,7 @@
                 part = jnp.exp(parts[j] - top)
                 added = jnp.sum(part, axis=-1, keepdims=True)
                 product = jnp.dot(
-                    part.astype(jnp.bfloat16), buf[s, 2, j], preferred_element_type=jnp.float32
+                    part.astype(jnp.bfloat16), buf[s, 1, j], preferred_element_type=jnp.float32
                 )
                 total = added if total is None else total + added
                 numer = product if numer is None else numer + product
@@ -222,19 +234,13 @@
     first = 2 * frame - (frame + n - 1) // n
     second = 2 * frame
     both = jnp.logical_and(frame > 0, frame < n - 1)
-    arrive(0)
-    attend(0, first, 0)
-
-    @pl.when(both)
-    def _():
-        arrive(1)
-        attend(1, second, 0)
-
-    for p in range(1, pieces):
+    for p in range(pieces):
+        arrive(0, p)
         attend(0, first, p)
 
         @pl.when(both)
         def _():
+            arrive(1, p)
             attend(1, second, p)
 
     load_weight.wait()
@@ -301,7 +307,7 @@
 
         @pl.when(frame != owner[h])
         def _():
-            for a in range(3):
+            for a in range(2 + pieces):
                 outgoing(h, a).wait_send()
 
     for i in range(n):
@@ -336,7 +342,8 @@
         scratch_shapes=[
             pltpu.SMEM(band_table.shape, jnp.int32),
             pltpu.SMEM(windows.shape, jnp.int32),
-            pltpu.VMEM((2, 3, n, length, HEAD), jnp.bfloat16),
+            pltpu.VMEM((2, pieces, n, 4, slab, HEAD), jnp.bfloat16),
+            pltpu.VMEM((2, 2, n, length, HEAD), jnp.bfloat16),
             pltpu.VMEM(out_weight.shape, jnp.bfloat16),
             pltpu.VMEM((2, pieces, n, 4 * slab, HEAD), jnp.bfloat16),
             pltpu.VMEM((pieces, 4 * slab, width), jnp.bfloat16),
@@ -346,8 +353,8 @@
             pltpu.VMEM((pieces, chunks, slab, part), jnp.bfloat16),
             pltpu.VMEM((pieces, chunks, slab, part), jnp.float32),
             pltpu.VMEM((chunks, 2 * slab, part), jnp.float32),
-            dma((heads, 3)),
-            dma((2, 3, n)),
+            dma((heads, 2 + pieces)),
+            dma((2, 2 + pieces, n)),
             dma((2, pieces, n)),
             dma((pieces, heads)),
             dma((pieces, chunks)),
@@ -360,7 +367,7 @@
         compiler_params=pltpu.CompilerParams(
             collective_id=0, has_side_effects=True, vmem_limit_bytes=60 * 1024 * 1024
         ),
-    )(queries, keys, values, band_table, windows, out_weight)
+    )(queries.reshape(4, block, width), keys, values, band_table, windows, out_weight)
     return mixed[None]
 
 

time: 55.9 us -> 53.6 us (0.959)
  Pallas kernels: 54 us -> 51.7 us
    pallas_call x1, Pallas kernels: 54 us -> 51.7 us  [fused(): pl.pallas_call(functools.partial(fused_kernel, n, pieces, chunks), out_sh...]
where the time goes in v3:
time: 53.6 us; the launch traced here: 53.4 us
  Pallas kernels  51.7 us (96%)
  local copies, waits for them, and re-layouts  1.77 us (3%)
    pallas_call x1, Pallas kernels, fused(): pl.pallas_call(functools.partial(fused_kernel, n, pieces, chunks), out_sh...  51.7 us
    unnamed x1, local copies, waits for them, and re-layouts  1.77 us

profile of v3, /device:TPU:0, one launch (start us, length us, event | category | flops | bytes accessed | tf_op | source)
XLA Modules:
  0.0 53.4 jit_solution(4387462627842789283)
XLA Ops:
  0.0 51.7 %shard_map.64 = bf16[64,3072]{1,0:T(8,128)(2,1)} custom-call(bf16[4,64,768]{2,1,0:T(8,128)(2,1)} %bitcast.3, bf16[1,256,768]{2,1,0:T(8,128)(2,1)} %k_hbm.1, bf16[1,256,768]{2,1,0:T(8,128)(2,1)} %v_hbm.1, s32[4,4]{1,0:T(4,128)} %band_hbm.1, s32[7]{0:T(128)} %windows_hbm.1, bf16[768,3072]{1,0:T(8,128)(2,1)} %w_hbm.1), custom_call_target="tpu_custom_call" | custom-call | tf_op jit(solution)/shard_map/pallas_call | solution.py:337
  51.7 1.8 %copy.8 = bf16[1,64,3072]{2,1,0:T(8,128)(2,1)} copy(bf16[1,64,3072]{2,1,0:T(8,128)(2,1)} %bitcast.2) | data formatting | bytes 786432

commit v4 on v3

--- a/solution.py
+++ b/solution.py
@@ -141,10 +141,8 @@
         for h in above:
             send_head(h, jnp.logical_not(low), which)
 
-    send_slot(0, (0, 1))
-    send_slot(1, (0, 1))
-    send_slot(0, (2,))
-    send_slot(1, (2,))
+    send_slot(0, (0, 1, 2))
+    send_slot(1, (0, 1, 2))
     for p in range(1, pieces):
         send_slot(0, (2 + p,))
         send_slot(1, (2 + p,))
@@ -328,7 +326,7 @@
     columns = out_weight.shape[1]
     heads = width // HEAD
     block = length // 4
-    chunks = 4
+    chunks = 2
     pieces = 2
     slab = block // pieces
     part = columns // chunks

time: 53.6 us -> 52.5 us (0.979)
  Pallas kernels: 51.7 us -> 50.6 us
    pallas_call x1, Pallas kernels: 51.7 us -> 50.6 us  [fused(): pl.pallas_call(functools.partial(fused_kernel, n, pieces, chunks), out_sh...]
where the time goes in v4:
time: 52.5 us; the launch traced here: 52.4 us
  Pallas kernels  50.6 us (96%)
  local copies, waits for them, and re-layouts  1.77 us (3%)
    pallas_call x1, Pallas kernels, fused(): pl.pallas_call(functools.partial(fused_kernel, n, pieces, chunks), out_sh...  50.6 us
    unnamed x1, local copies, waits for them, and re-layouts  1.77 us

profile of v4, /device:TPU:0, one launch (start us, length us, event | category | flops | bytes accessed | tf_op | source)
XLA Modules:
  0.0 52.4 jit_solution(5602494156963921134)
XLA Ops:
  0.0 50.6 %shard_map.64 = bf16[64,3072]{1,0:T(8,128)(2,1)} custom-call(bf16[4,64,768]{2,1,0:T(8,128)(2,1)} %bitcast.3, bf16[1,256,768]{2,1,0:T(8,128)(2,1)} %k_hbm.1, bf16[1,256,768]{2,1,0:T(8,128)(2,1)} %v_hbm.1, s32[4,4]{1,0:T(4,128)} %band_hbm.1, s32[7]{0:T(128)} %windows_hbm.1, bf16[768,3072]{1,0:T(8,128)(2,1)} %w_hbm.1), custom_call_target="tpu_custom_call" | custom-call | tf_op jit(solution)/shard_map/pallas_call | solution.py:335
  50.6 1.8 %copy.8 = bf16[1,64,3072]{2,1,0:T(8,128)(2,1)} copy(bf16[1,64,3072]{2,1,0:T(8,128)(2,1)} %bitcast.2) | data formatting | bytes 786432

commit v5 on v4

--- a/solution.py
+++ b/solution.py
@@ -141,11 +141,13 @@
         for h in above:
             send_head(h, jnp.logical_not(low), which)
 
-    send_slot(0, (0, 1, 2))
-    send_slot(1, (0, 1, 2))
+    send_slot(1, (0, 2))
+    send_slot(0, (0, 2))
+    send_slot(1, (1,))
+    send_slot(0, (1,))
     for p in range(1, pieces):
+        send_slot(1, (2 + p,))
         send_slot(0, (2 + p,))
-        send_slot(1, (2 + p,))
     for h in range(heads):
 
         @pl.when(frame == owner[h])
@@ -233,13 +235,13 @@
     second = 2 * frame
     both = jnp.logical_and(frame > 0, frame < n - 1)
     for p in range(pieces):
+        @pl.when(both)
+        def _():
+            arrive(1, p)
+            attend(1, second, p)
+
         arrive(0, p)
         attend(0, first, p)
-
-        @pl.when(both)
-        def _():
-            arrive(1, p)
-            attend(1, second, p)
 
     load_weight.wait()
     width = weight.shape[1] // chunks

time: 52.5 us -> 52.1 us (level)
  no operation moved by 1% of the time
where the time goes in v5:
time: 52.1 us; the launch traced here: 51.9 us
  Pallas kernels  50.2 us (96%)
  local copies, waits for them, and re-layouts  1.77 us (3%)
    pallas_call x1, Pallas kernels, fused(): pl.pallas_call(functools.partial(fused_kernel, n, pieces, chunks), out_sh...  50.2 us
    unnamed x1, local copies, waits for them, and re-layouts  1.77 us

profile of v5, /device:TPU:0, one launch (start us, length us, event | category | flops | bytes accessed | tf_op | source)
XLA Modules:
  0.0 51.9 jit_solution(1007402802743960783)
XLA Ops:
  0.0 50.2 %shard_map.64 = bf16[64,3072]{1,0:T(8,128)(2,1)} custom-call(bf16[4,64,768]{2,1,0:T(8,128)(2,1)} %bitcast.3, bf16[1,256,768]{2,1,0:T(8,128)(2,1)} %k_hbm.1, bf16[1,256,768]{2,1,0:T(8,128)(2,1)} %v_hbm.1, s32[4,4]{1,0:T(4,128)} %band_hbm.1, s32[7]{0:T(128)} %windows_hbm.1, bf16[768,3072]{1,0:T(8,128)(2,1)} %w_hbm.1), custom_call_target="tpu_custom_call" | custom-call | tf_op jit(solution)/shard_map/pallas_call | solution.py:337
  50.2 1.8 %copy.8 = bf16[1,64,3072]{2,1,0:T(8,128)(2,1)} copy(bf16[1,64,3072]{2,1,0:T(8,128)(2,1)} %bitcast.2) | data formatting | bytes 786432
